TPU v7x, 32 devices: a whole 2x2x4 slice. The times are simulated.
32 devices in a mesh: rows: 4 (over y, x), cols: 8 (over z, core).
Axes of the slice: x: 2, y: 2, z: 4, core: 2. Of those that a mesh axis runs over, the one named last changes fastest.
Arguments:
- object_tiles: float32 [2, 2, 3072, 6144], P(None, None, 'rows', 'cols'), may hold values from -6 to 6
- probe: float32 [2, 512, 512], replicated, may hold values from -6 to 6
- prop_phase: float32 [512, 512], replicated, may hold values from -3.140625 to 3.140625
- amplitudes: bfloat16 [4, 8, 1, 512, 512], P('rows', 'cols'), may hold values from 0 to 2
- offsets: int32 [4, 8, 1, 2], P('rows', 'cols'), may hold values from 0 to 512
- counts: int32 [4, 8], P('rows', 'cols'), may hold values from 0 to 1
- step_size: float32 [2], replicated, may hold values from 0.3 to 1
Outputs:
- updated: float32 [2, 2, 3072, 6144], P(None, None, 'rows', 'cols')
Inputs may be any that keep to these rules, and one draw needn't show every extreme that they name: `offsets`: row and column of a window's first cell in the device's tile extended by 128 cells on every side. `counts`: slots at or past a tile's count are ignored; a tile may have no probe position.
All inputs are finite; a program needn't handle non-finite values.
Results may differ from a plain program's by a relative error of at most 0.013.
The roundings to bfloat16 on the way count: a program that leaves them out, or rounds other values in their place, can miss the bound.
Values sent between devices are 32-bit elements; how exact they have to be, the bound alone decides.
A program may use at most 192 MiB of HBM per device.

v0:
```python
import functools
import math

import jax
import jax.numpy as jnp
import numpy as np
from jax import lax
from jax.experimental import pallas as pl
from jax.experimental.pallas import tpu as pltpu
from jax.sharding import PartitionSpec as P

H = 128
LANES = 128
SUBLANES = 8
ROWS = 512
F32 = jnp.float32
BF16 = jnp.bfloat16
MESH = pl.DeviceIdType.MESH


def dft_table(length):
    index = np.arange(length, dtype=np.int64)
    angles = ((index[:, None] * index[None, :]) % length).astype(np.float32) * np.float32(
        2.0 * math.pi / length
    )
    scaling = np.float32(1.0 / math.sqrt(length))
    return (
        jnp.asarray((np.cos(angles) * scaling).astype(BF16)),
        jnp.asarray((-np.sin(angles) * scaling).astype(BF16)),
    )


def make_tables(cos_ref, sin_ref, fwd, bwd):
    n = cos_ref.shape[0]
    c, s = cos_ref[...], sin_ref[...]
    for table, sine in ((fwd, s), (bwd, -s)):
        table[:n, :n] = c
        table[n:, n:] = c
        table[n:, :n] = sine
        table[:n, n:] = -sine


def transform(src, left, right, mid, epilogue):
    n = mid.shape[0]

    @pl.loop(0, n // ROWS)
    def _(i):
        at = pl.ds(pl.multiple_of(i * ROWS, ROWS), ROWS)
        low = pl.ds(pl.multiple_of(n + i * ROWS, ROWS), ROWS)
        mid[at, :n] = jnp.dot(left[at, :], src[...], preferred_element_type=F32).astype(BF16)
        mid[at, n:] = jnp.dot(left[low, :], src[...], preferred_element_type=F32).astype(BF16)

    @pl.loop(0, n // ROWS)
    def _(i):
        at = pl.ds(pl.multiple_of(i * ROWS, ROWS), ROWS)
        low = pl.ds(pl.multiple_of(n + i * ROWS, ROWS), ROWS)
        out = jnp.dot(mid[at, :], right[...], preferred_element_type=F32)
        epilogue(i, at, low, out[:, :n], out[:, n:])


class Copies:
    def __init__(self, sends, receives, locals_):
        self.sends, self.receives, self.locals = sends, receives, locals_
        self.remote_used = self.local_used = 0

    def remote(self, src, dst, there, here, device):
        k = self.remote_used
        self.remote_used += 1
        copy = pltpu.make_async_remote_copy(
            src_ref=src,
            dst_ref=dst,
            send_sem=self.sends.at[k],
            recv_sem=self.receives.at[k],
            device_id=device,
            device_id_type=MESH,
        )
        return Remote(copy, there, here)

    def local(self, src, dst):
        k = self.local_used
        self.local_used += 1
        return pltpu.make_async_copy(src, dst, self.locals.at[k])


class Remote:
    def __init__(self, copy, there, here):
        self.copy, self.there, self.here = copy, there, here

    def start(self):
        pl.when(self.there)(lambda: self.copy.start())

    def arrived(self):
        pl.when(self.here)(lambda: self.copy.wait_recv())

    def sent(self):
        pl.when(self.there)(lambda: self.copy.wait_send())


REMOTES = 2 + 2 * 18
LOCALS = 5 + 2 * 3 + 2 * 3


def step_kernel(
    offs_ref, count_ref, step_ref, meta, obj, probe_in, phase_in, amp_in, cos_in, sin_in, out,
    near, probe, k, amp, cos, sin, fwd, bwd, src, mid, psi,
    et0, et1, eb0, eb1, m0, m1, body0, body1, xs, xr, ss, sr, gz0, gz1,
    orr, ox, own_l, own_r, got_l, got_r, near_l, near_r,
    sends, receives, locals_,
):
    n = cos.shape[0]
    tile_rows, inner = obj.shape[2:]
    wide = inner + 2 * H
    tall = tile_rows + 2 * H
    half = (tall - n) // 2
    last = tile_rows - H
    ets, ebs, ms, bodies, gzs = (et0, et1), (eb0, eb1), (m0, m1), (body0, body1), (gz0, gz1)

    me_r, me_c = lax.axis_index("rows"), lax.axis_index("cols")
    n_r, n_c = lax.axis_size("rows"), lax.axis_size("cols")
    even = lax.rem(me_r, 2) == 0
    side = jnp.where(even, 1, -1)
    has_left, has_right = me_c > 0, me_c < n_c - 1
    has_above, has_below = me_r > 0, me_r < n_r - 1
    far_above, far_below = me_r > 1, me_r < n_r - 2
    row = lambda r: {"rows": r, "cols": me_c}
    col = lambda c: {"rows": me_r, "cols": c}
    partner = row(me_r + side)
    outward = row(me_r - 2 * side)
    inward = row(me_r + 2 * side)
    has_outward = jnp.where(even, me_r - 2, n_r - 3 - me_r) >= 0
    has_inward = jnp.where(even, n_r - 3 - me_r, me_r - 2) >= 0
    always = me_r >= 0

    copies = Copies(sends, receives, locals_)
    load_small = [
        copies.local(a, b)
        for a, b in ((cos_in, cos), (sin_in, sin), (probe_in, probe), (phase_in, k.at[0]), (amp_in.at[0, 0, 0], amp))
    ]
    load_edges, load_body = [], []
    centre = pl.ds(H, inner)
    for s in range(2):
        load_edges.append(
            [
                copies.local(obj.at[s, :, 0:H, :], ets[s].at[:, :, centre]),
                copies.local(obj.at[s, :, last : last + H, :], ebs[s].at[:, :, centre]),
            ]
        )
        load_body.append(copies.local(obj.at[s, :, H:last, :], ms[s].at[:, :, centre]))
    for c in load_edges[0] + load_edges[1]:
        c.start()
    for c in load_small[:2]:
        c.start()
    for c in load_body:
        c.start()
    for c in load_small[2:]:
        c.start()

    barrier = pltpu.get_barrier_semaphore()
    greeted = (
        (has_left, col(me_c - 1)), (has_right, col(me_c + 1)),
        (has_above, row(me_r - 1)), (has_below, row(me_r + 1)),
        (far_above, row(me_r - 2)), (far_below, row(me_r + 2)),
    )
    total = jnp.int32(0)
    for exists, device in greeted:
        total += exists.astype(jnp.int32)

        @pl.when(exists)
        def _(device=device):
            pl.semaphore_signal(barrier, inc=1, device_id=device, device_id_type=MESH)

    @pl.when(jnp.logical_not(has_left))
    def _():
        for ref in ets + ebs + ms:
            ref[:, :, :H] = jnp.zeros((2, ref.shape[1], H), F32)
        got_l[...] = jnp.zeros_like(got_l)
        near_l[...] = jnp.zeros_like(near_l)

    @pl.when(jnp.logical_not(has_right))
    def _():
        for ref in ets + ebs + ms:
            ref[:, :, H + inner :] = jnp.zeros((2, ref.shape[1], H), F32)
        got_r[...] = jnp.zeros_like(got_r)
        near_r[...] = jnp.zeros_like(near_r)

    @pl.when(jnp.logical_not(has_inward))
    def _():
        xr[...] = jnp.zeros_like(xr)

    @pl.when(jnp.logical_not(has_outward))
    def _():
        ox[...] = jnp.zeros_like(ox)

    @pl.when(jnp.logical_not(has_above))
    def _():
        near[0] = jnp.zeros(near.shape[1:], jnp.int32)

    @pl.when(jnp.logical_not(has_below))
    def _():
        near[1] = jnp.zeros(near.shape[1:], jnp.int32)

    pl.semaphore_wait(barrier, total)

    metas = [
        copies.remote(meta, near.at[0], has_below, has_above, row(me_r + 1)),
        copies.remote(meta, near.at[1], has_above, has_below, row(me_r - 1)),
    ]
    to_right = lambda a, b: copies.remote(a, b, has_right, has_left, col(me_c + 1))
    to_left = lambda a, b: copies.remote(a, b, has_left, has_right, col(me_c - 1))
    halo_edges, halo_body = [], []
    for s in range(2):
        both = []
        for ref, lo in ((ets[s], 0), (ebs[s], last)):
            both.append(to_right(obj.at[s, :, lo : lo + H, inner - H :], ref.at[:, :, 0:H]))
            both.append(to_left(obj.at[s, :, lo : lo + H, 0:H], ref.at[:, :, H + inner :]))
        halo_edges.append(both)
        halo_body.append(
            [
                to_right(obj.at[s, :, H:last, inner - H :], ms[s].at[:, :, 0:H]),
                to_left(obj.at[s, :, H:last, 0:H], ms[s].at[:, :, H + inner :]),
            ]
        )
    for c in metas + halo_edges[0] + halo_edges[1] + halo_body[0] + halo_body[1]:
        c.start()

    my_row, my_col = offs_ref[0], offs_ref[1]
    weight = jnp.where(count_ref[0] > 0, 1.0, 0.0).astype(F32)
    for c in metas:
        c.arrived()
    above_row, above_col = jnp.max(near[0, 0]), jnp.max(near[0, 1])
    below_row, below_col = jnp.max(near[1, 0]), jnp.max(near[1, 1])
    mate_row = jnp.where(even, below_row, above_row)
    mate_col = jnp.where(even, below_col, above_col)
    far_col = jnp.where(even, above_col, below_col)

    def take_columns(ref, part, at, start):
        return pltpu.roll(ref[part, at, :], lax.rem(wide - start, wide), axis=1)[:, :n]

    def take_rows(field, part, start, offset, height):
        strips = [field[part, q, pl.ds(start + offset, height), :] for q in range(n // LANES)]
        return jnp.concatenate(strips, axis=1)

    def put_rows(field, part, rows, value):
        for q in range(n // LANES):
            field[part, q, rows, :] = value[:, q * LANES : (q + 1) * LANES]

    every = pl.ds(0, H)

    outers, inners = [], []
    for s in range(2):
        outers.append([copies.remote(xs.at[s, p], xr.at[s, p], has_outward, has_inward, outward) for p in range(2)])
        inners.append([copies.remote(ss.at[s, p], sr.at[s, p], always, always, partner) for p in range(2)])
    for s in range(2):
        for c in load_edges[s]:
            c.wait()
        for c in halo_edges[s]:
            c.arrived()
        for p in range(2):
            top = take_columns(ets[s], p, every, far_col)
            bottom = take_columns(ebs[s], p, every, far_col)
            xs[s, p] = jnp.where(even, top, bottom)
            outers[s][p].start()
            top = take_columns(ets[s], p, every, mate_col)
            bottom = take_columns(ebs[s], p, every, mate_col)
            ss[s, p] = jnp.where(even, bottom, top)

    mate_near = jnp.where(even, mate_row <= half, mate_row > half)

    def pass_on(s, p):
        outers[s][p].arrived()
        ss[s, p] = jnp.where(mate_near, ss[s, p], xr[s, p])
        inners[s][p].start()

    for c in load_small:
        c.wait()
    make_tables(cos, sin, fwd, bwd)
    for gz in gzs:
        for lo, hi in ((0, tall - n - H), (tall - H, gz.shape[2])):

            @pl.loop(0, n // LANES)
            def _(q, gz=gz, lo=lo, hi=hi):
                for p in range(2):
                    gz[p, q, lo:hi, :] = jnp.zeros((hi - lo, LANES), F32)

    def fill_body(s):
        load_body[s].wait()
        for c in halo_body[s]:
            c.arrived()
        for p in range(2):
            put_rows(bodies[s], p, slice(H, 2 * H), take_columns(ets[s], p, every, my_col))
            put_rows(bodies[s], p, slice(H + last, 2 * H + last), take_columns(ebs[s], p, every, my_col))

            @pl.loop(0, (last - H) // H)
            def _(i, p=p):
                at = pl.ds(pl.multiple_of(i * H, H), H)
                to = pl.ds(pl.multiple_of(2 * H + i * H, H), H)
                put_rows(bodies[s], p, to, take_columns(ms[s], p, at, my_col))

    fill_body(0)

    @pl.loop(0, n // H)
    def _(i):
        at = pl.ds(pl.multiple_of(i * H, H), H)
        phase = k[0, at, :]
        k[1, at, :] = jnp.sin(phase)
        k[0, at, :] = jnp.cos(phase)

    pass_on(0, 0)
    pass_on(0, 1)
    fill_body(1)

    def halo_rows(s):
        for p in range(2):
            inners[s][p].arrived()
            block = sr[s, p]
            put_rows(bodies[s], p, slice(0, H), block)
            put_rows(bodies[s], p, slice(tall - H, tall), block)

    window = lambda s, p, offset, height: take_rows(bodies[s], p, my_row, offset, height)

    halo_rows(0)
    pass_on(1, 0)

    @pl.loop(0, n // H)
    def _(i):
        at = pl.ds(pl.multiple_of(i * H, H), H)
        low = pl.ds(pl.multiple_of(n + i * H, H), H)
        a_re = window(0, 0, i * H, H)
        a_im = window(0, 1, i * H, H)
        q_re, q_im = probe[0, at, :], probe[1, at, :]
        src[at, :] = (q_re * a_re - q_im * a_im).astype(BF16)
        src[low, :] = (q_re * a_im + q_im * a_re).astype(BF16)

    def propagate(i, at, low, re, im):
        k_re, k_im = k[0, at, :], k[1, at, :]
        src[at, :] = (re * k_re - im * k_im).astype(BF16)
        src[low, :] = (re * k_im + im * k_re).astype(BF16)

    def keep(i, at, low, re, im):
        psi[0, at, :] = re
        psi[1, at, :] = im

    transform(src, fwd, bwd, mid, propagate)
    pass_on(1, 1)
    transform(src, bwd, fwd, mid, keep)

    halo_rows(1)

    @pl.loop(0, n // H)
    def _(i):
        at = pl.ds(pl.multiple_of(i * H, H), H)
        low = pl.ds(pl.multiple_of(n + i * H, H), H)
        b_re = window(1, 0, i * H, H)
        b_im = window(1, 1, i * H, H)
        p_re, p_im = psi[0, at, :], psi[1, at, :]
        src[at, :] = (p_re * b_re - p_im * b_im).astype(BF16)
        src[low, :] = (p_re * b_im + p_im * b_re).astype(BF16)

    def detect(i, at, low, re, im):
        factor = 1.0 - amp[at, :].astype(F32) / jnp.sqrt(re * re + im * im + 1.0)
        src[at, :] = (re * factor).astype(BF16)
        src[low, :] = (im * factor).astype(BF16)

    first_row = tall - n - H

    def spread(i, at, low, re, im):
        p_re, p_im = psi[0, at, :], psi[1, at, :]
        b_re = window(1, 0, i * ROWS, ROWS)
        b_im = window(1, 1, i * ROWS, ROWS)
        to = pl.ds(pl.multiple_of(first_row + i * ROWS, SUBLANES), ROWS)
        put_rows(gz1, 0, to, weight * (p_re * re + p_im * im))
        put_rows(gz1, 1, to, weight * (p_re * im - p_im * re))
        src[at, :] = (b_re * re + b_im * im).astype(BF16)
        src[low, :] = (b_re * im - b_im * re).astype(BF16)

    transform(src, fwd, bwd, mid, detect)
    transform(src, bwd, fwd, mid, spread)

    spills, relays = [], []
    for s in range(2):
        spills.append([copies.remote(ss.at[s, p], orr.at[s, p], always, always, partner) for p in range(2)])
        relays.append([copies.remote(orr.at[s, p], ox.at[s, p], has_inward, has_outward, inward) for p in range(2)])

    def spill(s):
        start = jnp.where(my_row <= half, first_row - my_row, first_row + tile_rows + H - my_row)
        for p in range(2):
            inners[s][p].sent()
            ss[s, p] = take_rows(gzs[s], p, start, 0, H)
            spills[s][p].start()

    def relay(s, p):
        spills[s][p].arrived()
        relays[s][p].start()

    def back(i, at, low, re, im):
        k_re, k_im = k[0, at, :], k[1, at, :]
        src[at, :] = (re * k_re + im * k_im).astype(BF16)
        src[low, :] = (im * k_re - re * k_im).astype(BF16)

    def finish(i, at, low, re, im):
        q_re, q_im = probe[0, at, :], probe[1, at, :]
        to = pl.ds(pl.multiple_of(first_row + i * ROWS, SUBLANES), ROWS)
        put_rows(gz0, 0, to, weight * (q_re * re + q_im * im))
        put_rows(gz0, 1, to, weight * (q_re * im - q_im * re))

    spill(1)
    transform(src, fwd, bwd, mid, back)
    relay(1, 0)
    transform(src, bwd, fwd, mid, finish)
    spill(0)
    relay(1, 1)

    spread_out = lambda block, start: pltpu.roll(
        jnp.concatenate([block, jnp.zeros((block.shape[0], wide - n), F32)], axis=1), start, axis=1
    )

    def place_rows(s, p, ref, offset, at):
        block = spread_out(take_rows(gzs[s], p, tall - n - my_row, offset, H), my_col)
        rows = pl.ds(pl.multiple_of(offset, H), H)
        own_l[s, p, rows, :] = block[:, :H]
        own_r[s, p, rows, :] = block[:, H + inner :]
        ref[p, at, H : H + inner] -= step_ref[s] * block[:, H : H + inner]

    early, lates = [], []
    for s in range(2):
        early.append([to_left(own_l.at[s], got_r.at[s]), to_right(own_r.at[s], got_l.at[s])])
        lates.append([to_left(xs.at[s, :, :, : 2 * H], near_r.at[s]), to_right(xs.at[s, :, :, 2 * H : 4 * H], near_l.at[s])])

    def place_own(s):
        for p in range(2):
            place_rows(s, p, ets[s], 0, every)
            place_rows(s, p, ebs[s], last, every)

            @pl.loop(0, (last - H) // H)
            def _(i, p=p):
                place_rows(s, p, ms[s], H + i * H, pl.ds(pl.multiple_of(i * H, H), H))

        for c in early[s]:
            c.start()

    def place_near(s):
        for p in range(2):
            relays[s][p].arrived()
            outers[s][p].sent()
        for p in range(2):
            for ref, e, mine, start in (
                (ets[s], 0, jnp.logical_and(has_above, above_row > half), above_col),
                (ebs[s], 1, jnp.logical_and(has_below, below_row <= half), below_col),
            ):
                outer = even if e == 0 else jnp.logical_not(even)
                block = jnp.where(outer, ox[s, p], orr[s, p])
                block = spread_out(jnp.where(mine, block, jnp.zeros_like(block)), start)
                xs[s, p, :, e * H : (e + 1) * H] = block[:, :H]
                xs[s, p, :, (2 + e) * H : (3 + e) * H] = block[:, H + inner :]
                ref[p, :, H : H + inner] -= step_ref[s] * block[:, H : H + inner]
        for c in lates[s]:
            c.start()

    outs = []
    for s in range(2):
        outs.append(
            [
                copies.local(ms[s].at[:, :, centre], out.at[s, :, H:last, :]),
                copies.local(ets[s].at[:, :, centre], out.at[s, :, 0:H, :]),
                copies.local(ebs[s].at[:, :, centre], out.at[s, :, last : last + H, :]),
            ]
        )

    def sides_body(s):
        for c in early[s]:
            c.arrived()
        for p in range(2):

            @pl.loop(0, (last - H) // H)
            def _(i, p=p):
                at = pl.ds(pl.multiple_of(i * H, H), H)
                rows = pl.ds(pl.multiple_of(H + i * H, H), H)
                ms[s][p, at, H : 2 * H] -= step_ref[s] * got_l[s, p, rows, :]
                ms[s][p, at, inner : H + inner] -= step_ref[s] * got_r[s, p, rows, :]

        outs[s][0].start()

    def sides_edges(s):
        for c in lates[s]:
            c.arrived()
        for p in range(2):
            for ref, e, lo in ((ets[s], 0, 0), (ebs[s], 1, last)):
                ref[p, :, H : 2 * H] -= step_ref[s] * (got_l[s, p, lo : lo + H, :] + near_l[s, p, :, e * H : (e + 1) * H])
                ref[p, :, inner : H + inner] -= step_ref[s] * (got_r[s, p, lo : lo + H, :] + near_r[s, p, :, e * H : (e + 1) * H])
        for c in outs[s][1:]:
            c.start()

    place_own(1)
    relay(0, 0)
    place_own(0)
    relay(0, 1)
    place_near(1)
    sides_body(1)
    sides_body(0)
    sides_edges(1)
    place_near(0)
    sides_edges(0)

    for group in [metas] + halo_edges + halo_body + spills + relays + early + lates:
        for c in group:
            c.sent()
    for group in outs:
        for c in group:
            c.wait()
    assert copies.remote_used == REMOTES and copies.local_used == LOCALS


def per_device(object_tiles, probe, prop_phase, amplitudes, offsets, counts, step_size):
    n = probe.shape[1]
    rows, inner = object_tiles.shape[2:]
    cos, sin = dft_table(n)
    mine = offsets[0, 0, 0]
    meta = jnp.broadcast_to(mine[:, None, None], (2, SUBLANES, LANES))
    tall, wide = rows + 2 * H, inner + 2 * H
    smem = pl.BlockSpec(memory_space=pltpu.SMEM)
    anywhere = pl.BlockSpec(memory_space=pl.ANY)
    vmem = lambda *shape, kind=F32: pltpu.VMEM(shape, kind)
    edge, body = vmem(2, H, wide), vmem(2, rows - 2 * H, wide)
    strip, late = vmem(2, 2, rows, H), vmem(2, 2, H, 2 * H)
    block = vmem(2, 2, H, n)
    gz = vmem(2, n // LANES, 2 * tall - n - 2 * H, LANES)
    scratch = (
        [vmem(2, 2, SUBLANES, LANES, kind=jnp.int32), vmem(2, n, n), vmem(2, n, n), vmem(n, n, kind=BF16)]
        + [vmem(n, n, kind=BF16)] * 2
        + [vmem(2 * n, 2 * n, kind=BF16)] * 2
        + [vmem(2 * n, n, kind=BF16), vmem(n, 2 * n, kind=BF16), vmem(2, n, n)]
        + [edge] * 4
        + [body] * 2
        + [vmem(2, n // LANES, tall, LANES)] * 2
        + [block] * 4
        + [gz] * 2
        + [block] * 2
        + [strip] * 4
        + [late] * 2
        + [pltpu.SemaphoreType.DMA((REMOTES,))] * 2
        + [pltpu.SemaphoreType.DMA((LOCALS,))]
    )
    return pl.pallas_call(
        step_kernel,
        in_specs=[smem] * 3 + [anywhere] * 7,
        out_specs=anywhere,
        out_shape=jax.ShapeDtypeStruct(object_tiles.shape, F32),
        scratch_shapes=scratch,
        name="step",
        compiler_params=pltpu.CompilerParams(
            collective_id=0, has_side_effects=True, vmem_limit_bytes=67043328
        ),
    )(mine, counts[0], step_size, meta, object_tiles, probe, prop_phase, amplitudes, cos, sin)


def solution(mesh):
    return jax.shard_map(
        per_device,
        mesh=mesh,
        in_specs=(
            P(None, None, "rows", "cols"),
            P(),
            P(),
            P("rows", "cols", None, None, None),
            P("rows", "cols", None, None),
            P("rows", "cols"),
            P(),
        ),
        out_specs=P(None, None, "rows", "cols"),
        check_vma=False,
    )
```

profile of v0, /device:TPU:12, one launch (start us, length us, event | category | flops | bytes accessed | tf_op | source)
XLA Modules:
  0.0 110.8 jit_solution(12653491897233047417)
XLA Ops:
  0.7 1.3 %broadcast_in_dim.2.meta = s32[2,8,128]{2,1,0:T(8,128)} broadcast(s32[2]{0:T(128)} %bitcast.3), dimensions={0} | broadcast | bytes 8200 | tf_op jit(solution)/shard_map/broadcast_in_dim | solution.py:518
  2.0 100.8 %step.1 = f32[2,2,768,768]{3,2,1,0:T(8,128)} custom-call(s32[2]{0:T(128)} %bitcast.4, s32[1]{0:T(128)} %bitcast.2.count_ref, f32[2]{0:T(128)} %step_ref.1, s32[2,8,128]{2,1,0:T(8,128)} %broadcast_in_dim.2.meta, f32[2,2,768,768]{3,2,1,0:T(8,128)} %obj.1, f32[2,512,512]{2,1,0:T(8,128)} %probe_in.1, f32[512,512]{1,0:T(8,128)} %phase_in.1, ...), custom_call_target="tpu_custom_call" | custom-call | tf_op jit(solution)/shard_map/step/pallas_call | solution.py:543
  102.8 8.0 %copy.12 = f32[2,2,768,768]{3,2,1,0:T(8,128)} copy(f32[2,2,768,768]{3,2,1,0:T(8,128)} %step.1) | data formatting | bytes 18874368
where the time goes:
time: 111 us
  Pallas kernels  101 us (91%)
  local copies, waits for them, and re-layouts  9.35 us (8%)
    pallas_call x1, Pallas kernels, per_device(): pl.pallas_call(step_kernel, in_specs=[smem] * 3 + [anywhere] * 7, out_spe...  101 us
    unnamed x1, local copies, waits for them, and re-layouts  8.03 us

commit v1 on v0

v1 whole, which is shorter than its diff:
```python
import math

import jax
import jax.numpy as jnp
import numpy as np
from jax import lax
from jax.experimental import pallas as pl
from jax.experimental.pallas import tpu as pltpu
from jax.sharding import PartitionSpec as P

H = 128
LANES = 128
SUBLANES = 8
PARTS = 2
F32 = jnp.float32
BF16 = jnp.bfloat16
MESH = pl.DeviceIdType.MESH


def dft_table(length):
    index = np.arange(length, dtype=np.int64)
    angles = ((index[:, None] * index[None, :]) % length).astype(np.float32) * np.float32(
        2.0 * math.pi / length
    )
    scaling = np.float32(1.0 / math.sqrt(length))
    return (
        jnp.asarray((np.cos(angles) * scaling).astype(BF16)),
        jnp.asarray((-np.sin(angles) * scaling).astype(BF16)),
    )


def make_tables(cos_ref, sin_ref, fwd, bwd):
    n = cos_ref.shape[0]
    c, s = cos_ref[...], sin_ref[...]
    for table, sine in ((fwd, s), (bwd, -s)):
        table[:n, :n] = c
        table[n:, n:] = c
        table[n:, :n] = sine
        table[:n, n:] = -sine


class Copies:
    def __init__(self, sends, receives, locals_):
        self.sends, self.receives, self.locals = sends, receives, locals_
        self.remotes = []
        self.local_used = 0

    def remote(self, src, dst, there, here, device):
        k = len(self.remotes)
        copy = pltpu.make_async_remote_copy(
            src_ref=src,
            dst_ref=dst,
            send_sem=self.sends.at[k],
            recv_sem=self.receives.at[k],
            device_id=device,
            device_id_type=MESH,
        )
        self.remotes.append(Remote(copy, there, here))
        return self.remotes[-1]

    def local(self, src, dst):
        k = self.local_used
        self.local_used += 1
        return pltpu.make_async_copy(src, dst, self.locals.at[k])


class Remote:
    def __init__(self, copy, there, here):
        self.copy, self.there, self.here = copy, there, here
        self.waited = False

    def start(self):
        pl.when(self.there)(lambda: self.copy.start())

    def arrived(self):
        pl.when(self.here)(lambda: self.copy.wait_recv())

    def sent(self):
        self.waited = True
        pl.when(self.there)(lambda: self.copy.wait_send())


REMOTES = 4 + 2 * (8 + 12 * PARTS)
LOCALS = 5 + 2 * 3


def step_kernel(
    offs_ref, count_ref, step_ref, obj, probe_in, phase_in, amp_in, cos_in, sin_in, out,
    meta, near, probe, k, amp, cos, sin, fwd, bwd, src, mid, psi,
    hl, hr, body0, body1, xs, xr, ss, sr, gz0, gz1,
    orr, ox, own_l, own_r, gl0, gl1, gr0, gr1, near_l, near_r,
    sends, receives, locals_,
):
    n = cos.shape[0]
    tile_rows, inner = obj.shape[2:]
    wide = inner + 2 * H
    tall = tile_rows + 2 * H
    half = (tall - n) // 2
    last = tile_rows - H
    bodies, gzs, gls, grs = (body0, body1), (gz0, gz1), (gl0, gl1), (gr0, gr1)

    me_r, me_c = lax.axis_index("rows"), lax.axis_index("cols")
    n_r, n_c = lax.axis_size("rows"), lax.axis_size("cols")
    odd = lax.rem(me_r, 2)
    even = odd == 0
    side = 1 - 2 * odd
    has_left, has_right = me_c > 0, me_c < n_c - 1
    has_above, has_below = me_r > 0, me_r < n_r - 1
    far_above, far_below = me_r > 1, me_r < n_r - 2
    row = lambda r: {"rows": r, "cols": me_c}
    col = lambda c: {"rows": me_r, "cols": c}
    partner = row(me_r + side)
    outward = row(me_r - 2 * side)
    inward = row(me_r + 2 * side)
    has_outward = jnp.where(even, me_r - 2, n_r - 3 - me_r) >= 0
    has_inward = jnp.where(even, n_r - 3 - me_r, me_r - 2) >= 0
    always = me_r >= 0

    copies = Copies(sends, receives, locals_)
    far_rows = pl.ds(pl.multiple_of(odd * last, H), H)
    mate_rows = pl.ds(pl.multiple_of((1 - odd) * last, H), H)
    mid_rows = pl.ds(H, last - H)
    pieces = (far_rows, mate_rows, mid_rows)

    loads = [[copies.local(obj.at[s, :, at, :], out.at[s, :, at, :]) for at in pieces] for s in range(2)]
    load_small = [
        copies.local(a, b)
        for a, b in ((cos_in, cos), (sin_in, sin), (phase_in, k.at[0]), (probe_in, probe), (amp_in.at[0, 0, 0], amp))
    ]
    for c in loads[0][:2] + loads[1][:2] + load_small[:3] + loads[0][2:] + load_small[3:] + loads[1][2:]:
        c.start()
    for i in range(2):
        meta[i] = jnp.full(meta.shape[1:], offs_ref[i], jnp.int32)

    barrier = pltpu.get_barrier_semaphore()
    greeted = (
        (has_left, col(me_c - 1)), (has_right, col(me_c + 1)),
        (has_above, row(me_r - 1)), (has_below, row(me_r + 1)),
        (far_above, row(me_r - 2)), (far_below, row(me_r + 2)),
    )
    total = jnp.int32(0)
    for exists, device in greeted:
        total += exists.astype(jnp.int32)

        @pl.when(exists)
        def _(device=device):
            pl.semaphore_signal(barrier, inc=1, device_id=device, device_id_type=MESH)

    first_row = tall - n - H

    @pl.when(jnp.logical_not(has_left))
    def _():
        hl[...] = jnp.zeros_like(hl)
        near_l[...] = jnp.zeros_like(near_l)
        for ref in gls:
            ref[:, first_row : first_row + n, :] = jnp.zeros((2, n, H), F32)

    @pl.when(jnp.logical_not(has_right))
    def _():
        hr[...] = jnp.zeros_like(hr)
        near_r[...] = jnp.zeros_like(near_r)
        for ref in grs:
            ref[:, first_row : first_row + n, :] = jnp.zeros((2, n, H), F32)

    @pl.when(jnp.logical_not(has_inward))
    def _():
        xr[...] = jnp.zeros_like(xr)

    @pl.when(jnp.logical_not(has_outward))
    def _():
        ox[...] = jnp.zeros_like(ox)

    for i, exists in enumerate((has_above, has_below, has_left, has_right)):

        @pl.when(jnp.logical_not(exists))
        def _(i=i):
            near[i] = jnp.zeros(near.shape[1:], jnp.int32)

    pl.semaphore_wait(barrier, total)

    to_right = lambda a, b: copies.remote(a, b, has_right, has_left, col(me_c + 1))
    to_left = lambda a, b: copies.remote(a, b, has_left, has_right, col(me_c - 1))
    metas = [
        copies.remote(meta, near.at[0], has_below, has_above, row(me_r + 1)),
        copies.remote(meta, near.at[1], has_above, has_below, row(me_r - 1)),
        to_right(meta, near.at[2]),
        to_left(meta, near.at[3]),
    ]
    halos = [
        [
            [
                to_right(obj.at[s, :, at, inner - H :], hl.at[s, :, at, :]),
                to_left(obj.at[s, :, at, 0:H], hr.at[s, :, at, :]),
            ]
            for at in pieces
        ]
        for s in range(2)
    ]
    for group in (metas, halos[0][0], halos[0][1], halos[1][0], halos[1][1], halos[0][2], halos[1][2]):
        for c in group:
            c.start()

    for lo, hi in ((0, first_row), (first_row + n, gz0.shape[2])):

        @pl.loop(0, n // LANES)
        def _(q, lo=lo, hi=hi):
            for gz in gzs:
                for p in range(2):
                    gz[p, q, lo:hi, :] = jnp.zeros((hi - lo, LANES), F32)

        for ref in gls + grs:
            ref[:, lo:hi, :] = jnp.zeros((2, hi - lo, H), F32)

    my_row, my_col = offs_ref[0], offs_ref[1]
    weight = jnp.where(count_ref[0] > 0, 1.0, 0.0).astype(F32)
    for c in metas:
        c.arrived()
    above_row, above_col = jnp.max(near[0, 0]), jnp.max(near[0, 1])
    below_row, below_col = jnp.max(near[1, 0]), jnp.max(near[1, 1])
    left_row, right_row = jnp.max(near[2, 0]), jnp.max(near[3, 0])
    mate_row = jnp.where(even, below_row, above_row)
    mate_col = jnp.where(even, below_col, above_col)
    far_col = jnp.where(even, above_col, below_col)

    def take_columns(s, p, at, start):
        line = jnp.concatenate([hl[s, p, at, :], out[s, p, at, :], hr[s, p, at, :]], axis=1)
        return pltpu.roll(line, lax.rem(wide - start, wide), axis=1)[:, :n]

    def take_rows(field, part, start, height):
        strips = [field[part, q, pl.ds(start, height), :] for q in range(n // LANES)]
        return jnp.concatenate(strips, axis=1)

    def put_rows(field, part, rows, value):
        for q in range(n // LANES):
            field[part, q, rows, :] = value[:, q * LANES : (q + 1) * LANES]

    size = H // PARTS
    chunks = [(p, h) for p in range(2) for h in range(PARTS)]
    lines = lambda h: pl.ds(h * size, size)

    outers = [
        {(p, h): copies.remote(xs.at[s, p, lines(h)], xr.at[s, p, lines(h)], has_outward, has_inward, outward) for p, h in chunks}
        for s in range(2)
    ]
    inners = [
        {(p, h): copies.remote(ss.at[s, p, lines(h)], sr.at[s, p, lines(h)], always, always, partner) for p, h in chunks}
        for s in range(2)
    ]
    for s in range(2):
        loads[s][0].wait()
        for c in halos[s][0]:
            c.arrived()
        for p, h in chunks:
            at = pl.ds(pl.multiple_of(odd * last + h * size, size), size)
            xs[s, p, lines(h)] = take_columns(s, p, at, far_col)
            outers[s][p, h].start()
    for s in range(2):
        loads[s][1].wait()
        for c in halos[s][1]:
            c.arrived()
        for p in range(2):
            ss[s, p] = take_columns(s, p, mate_rows, mate_col)

    mate_near = jnp.where(even, mate_row <= half, mate_row > half)

    def pass_on(s, i):
        p, h = chunks[i]
        outers[s][p, h].arrived()
        ss[s, p, lines(h)] = jnp.where(mate_near, ss[s, p, lines(h)], xr[s, p, lines(h)])
        inners[s][p, h].start()

    for c in load_small[:3]:
        c.wait()

    def propagator(lo, hi):
        @pl.loop(lo // LANES, hi // LANES)
        def _(i):
            at = pl.ds(pl.multiple_of(i * LANES, LANES), LANES)
            phase = k[0, at, :]
            k[1, at, :] = jnp.sin(phase)
            k[0, at, :] = jnp.cos(phase)

    def fill_body(s, p):
        for lo in (0, last):
            put_rows(bodies[s], p, slice(H + lo, 2 * H + lo), take_columns(s, p, slice(lo, lo + H), my_col))

        @pl.loop(0, (last - H) // H)
        def _(i):
            at = pl.ds(pl.multiple_of(H + i * H, H), H)
            to = pl.ds(pl.multiple_of(2 * H + i * H, H), H)
            put_rows(bodies[s], p, to, take_columns(s, p, at, my_col))

    def body_ready(s):
        loads[s][2].wait()
        for c in halos[s][2]:
            c.arrived()

    count = len(chunks)
    make_tables(cos, sin, fwd, bwd)
    pass_on(0, 0)
    propagator(0, n // 2)
    pass_on(0, 1)
    propagator(n // 2, n)
    body_ready(0)
    for i in range(2, count):
        pass_on(0, i)
        if i < 4:
            fill_body(0, i - 2)
    for c in load_small[3:]:
        c.wait()

    def halo_rows(s):
        for p, h in chunks:
            inners[s][p, h].arrived()
        for p in range(2):
            block = sr[s, p]
            put_rows(bodies[s], p, slice(0, H), block)
            put_rows(bodies[s], p, slice(tall - H, tall), block)

    window = lambda s, p, lo, height: take_rows(bodies[s], p, my_row + lo, height)
    full = lambda lo, height: (pl.ds(lo, height), pl.ds(n + lo, height))

    def stage_one(left, between=()):
        for i in range(2):
            mid[:, i * n : (i + 1) * n] = jnp.dot(
                left[i * n : (i + 1) * n, :], src[...], preferred_element_type=F32
            ).astype(BF16)
            for f in between[i : i + 1]:
                f()

    def stage_two(right, spans, epilogue):
        rows = [mid[lo : lo + height, :] for lo, height in spans]
        rows = rows[0] if len(rows) == 1 else jnp.concatenate(rows, axis=0)
        result = jnp.dot(rows, right[...], preferred_element_type=F32)
        at = 0
        for lo, height in spans:
            epilogue(lo, height, result[at : at + height, :n], result[at : at + height, n:])
            at += height

    whole = [(0, n)]
    ends = [(0, H), (n - H, H)]
    middle = [(H, n - 2 * H)]

    halo_rows(0)
    pass_on(1, 0)

    @pl.loop(0, n // H)
    def _(i):
        at = pl.ds(pl.multiple_of(i * H, H), H)
        low = pl.ds(pl.multiple_of(n + i * H, H), H)
        a_re = window(0, 0, i * H, H)
        a_im = window(0, 1, i * H, H)
        q_re, q_im = probe[0, at, :], probe[1, at, :]
        src[at, :] = (q_re * a_re - q_im * a_im).astype(BF16)
        src[low, :] = (q_re * a_im + q_im * a_re).astype(BF16)

    def propagate(lo, height, re, im):
        at, low = full(lo, height)
        k_re, k_im = k[0, at, :], k[1, at, :]
        src[at, :] = (re * k_re - im * k_im).astype(BF16)
        src[low, :] = (re * k_im + im * k_re).astype(BF16)

    def keep(lo, height, re, im):
        at, _ = full(lo, height)
        psi[0, at, :] = re
        psi[1, at, :] = im

    stage_one(fwd, (lambda: pass_on(1, 1),))
    stage_two(bwd, whole, propagate)
    for i in range(2, count // 2 + 1):
        pass_on(1, i)
    stage_one(bwd)
    body_ready(1)
    fill_body(1, 0)
    for i in range(count // 2 + 1, count):
        pass_on(1, i)
    stage_two(fwd, whole, keep)
    fill_body(1, 1)

    halo_rows(1)

    @pl.loop(0, n // H)
    def _(i):
        at = pl.ds(pl.multiple_of(i * H, H), H)
        low = pl.ds(pl.multiple_of(n + i * H, H), H)
        b_re = window(1, 0, i * H, H)
        b_im = window(1, 1, i * H, H)
        p_re, p_im = psi[0, at, :], psi[1, at, :]
        src[at, :] = (p_re * b_re - p_im * b_im).astype(BF16)
        src[low, :] = (p_re * b_im + p_im * b_re).astype(BF16)

    def detect(lo, height, re, im):
        at, low = full(lo, height)
        factor = 1.0 - amp[at, :].astype(F32) / jnp.sqrt(re * re + im * im + 1.0)
        src[at, :] = (re * factor).astype(BF16)
        src[low, :] = (im * factor).astype(BF16)

    def emit(s, p, lo, height, value):
        put_rows(gzs[s], p, pl.ds(first_row + lo, height), value)
        lane = lax.broadcasted_iota(jnp.int32, (height, LANES), 1)
        turn = lax.rem(my_col, LANES)
        at = pl.ds(lo, height)
        own_l[s, p, at, :] = jnp.where(lane >= my_col, pltpu.roll(value[:, :LANES], turn, axis=1), 0.0)
        own_r[s, p, at, :] = jnp.where(
            lane < my_col - (inner + H - n), pltpu.roll(value[:, n - LANES :], turn, axis=1), 0.0
        )

    def spread(lo, height, re, im):
        at, low = full(lo, height)
        p_re, p_im = psi[0, at, :], psi[1, at, :]
        b_re = window(1, 0, lo, height)
        b_im = window(1, 1, lo, height)
        emit(1, 0, lo, height, weight * (p_re * re + p_im * im))
        emit(1, 1, lo, height, weight * (p_re * im - p_im * re))
        src[at, :] = (b_re * re + b_im * im).astype(BF16)
        src[low, :] = (b_re * im - b_im * re).astype(BF16)

    spills = [
        {(p, h): copies.remote(ss.at[s, p, lines(h)], orr.at[s, p, lines(h)], always, always, partner) for p, h in chunks}
        for s in range(2)
    ]
    relays = [
        {(p, h): copies.remote(orr.at[s, p, lines(h)], ox.at[s, p, lines(h)], has_inward, has_outward, inward) for p, h in chunks}
        for s in range(2)
    ]
    early = [
        [
            to_left(own_l.at[s], grs[s].at[:, first_row : first_row + n, :]),
            to_right(own_r.at[s], gls[s].at[:, first_row : first_row + n, :]),
        ]
        for s in range(2)
    ]
    lates = [
        {
            (p, h): [
                to_left(xs.at[s, p, lines(h), : 2 * H], near_r.at[s, p, lines(h)]),
                to_right(xs.at[s, p, lines(h), 2 * H : 4 * H], near_l.at[s, p, lines(h)]),
            ]
            for p, h in chunks
        }
        for s in range(2)
    ]

    def spill(s):
        start = jnp.where(my_row <= half, first_row - my_row, first_row + tile_rows + H - my_row)
        for p, h in chunks:
            inners[s][p, h].sent()
            ss[s, p, lines(h)] = take_rows(gzs[s], p, start + h * size, size)
            spills[s][p, h].start()

    def relay(s, i):
        spills[s][chunks[i]].arrived()
        relays[s][chunks[i]].start()

    def back(lo, height, re, im):
        at, low = full(lo, height)
        k_re, k_im = k[0, at, :], k[1, at, :]
        src[at, :] = (re * k_re + im * k_im).astype(BF16)
        src[low, :] = (im * k_re - re * k_im).astype(BF16)

    def finish(lo, height, re, im):
        at, _ = full(lo, height)
        q_re, q_im = probe[0, at, :], probe[1, at, :]
        emit(0, 0, lo, height, weight * (q_re * re + q_im * im))
        emit(0, 1, lo, height, weight * (q_re * im - q_im * re))

    stage_one(fwd)
    stage_two(bwd, whole, detect)
    stage_one(bwd)
    stage_two(fwd, ends, spread)
    spill(1)
    stage_two(fwd, middle, spread)
    for c in early[1]:
        c.start()
    stage_one(fwd)
    relay(1, 0)
    stage_two(bwd, whole, back)
    for i in range(1, count // 2):
        relay(1, i)
    stage_one(bwd)
    stage_two(fwd, ends, finish)
    spill(0)
    stage_two(fwd, middle, finish)
    for c in early[0]:
        c.start()

    spread_out = lambda block, start: pltpu.roll(
        jnp.concatenate([block, jnp.zeros((block.shape[0], wide - n), F32)], axis=1), start, axis=1
    )

    def place_own(s, p):
        @pl.loop(0, tile_rows // H)
        def _(i):
            block = spread_out(take_rows(gzs[s], p, tall - n - my_row + i * H, H), my_col)
            at = pl.ds(pl.multiple_of(i * H, H), H)
            out[s, p, at, :] -= step_ref[s] * block[:, H : H + inner]

    def place_near(s, i):
        p, h = chunks[i]
        relays[s][p, h].arrived()
        outers[s][p, h].sent()
        for e, mine, start in (
            (0, jnp.logical_and(has_above, above_row > half), above_col),
            (1, jnp.logical_and(has_below, below_row <= half), below_col),
        ):
            outer = even if e == 0 else jnp.logical_not(even)
            block = jnp.where(outer, ox[s, p, lines(h)], orr[s, p, lines(h)])
            block = spread_out(jnp.where(mine, block, jnp.zeros_like(block)), start)
            xs[s, p, lines(h), e * H : (e + 1) * H] = block[:, :H]
            xs[s, p, lines(h), (2 + e) * H : (3 + e) * H] = block[:, H + inner :]
            at = pl.ds(e * last + h * size, size)
            out[s, p, at, :] -= step_ref[s] * block[:, H : H + inner]
        for c in lates[s][p, h]:
            c.start()

    def sides(s):
        for c in early[s]:
            c.arrived()
        for p in range(2):

            @pl.loop(0, tile_rows // H)
            def _(i, p=p):
                at = pl.ds(pl.multiple_of(i * H, H), H)
                from_left = gls[s][p, pl.ds(tall - n - left_row + i * H, H), :]
                from_right = grs[s][p, pl.ds(tall - n - right_row + i * H, H), :]
                out[s, p, at, :H] -= step_ref[s] * from_left
                out[s, p, at, inner - H :] -= step_ref[s] * from_right

    def corners(s, i):
        p, h = chunks[i]
        for c in lates[s][p, h]:
            c.arrived()
        for e in range(2):
            at = pl.ds(e * last + h * size, size)
            out[s, p, at, :H] -= step_ref[s] * near_l[s, p, lines(h), e * H : (e + 1) * H]
            out[s, p, at, inner - H :] -= step_ref[s] * near_r[s, p, lines(h), e * H : (e + 1) * H]

    for i in range(count // 2, count):
        relay(1, i)
    place_own(1, 0)
    place_own(1, 1)
    for i in range(count):
        place_near(1, i)
    relay(0, 0)
    place_own(0, 0)
    relay(0, 1)
    place_own(0, 1)
    sides(1)
    for i in range(2, count):
        relay(0, i)
        place_near(0, i - 2)
    for i in range(count):
        corners(1, i)
    sides(0)
    for i in range(count - 2, count):
        place_near(0, i)
    for i in range(count):
        corners(0, i)

    for c in copies.remotes:
        if not c.waited:
            c.sent()
    assert len(copies.remotes) == REMOTES and copies.local_used == LOCALS


def write_kernel(done, out, sems):
    copies = []
    for s in range(2):
        for p in range(2):
            copies.append(pltpu.make_async_copy(done.at[s, p], out.at[s, p], sems.at[2 * s + p]))
    for c in copies:
        c.start()
    for c in copies:
        c.wait()


def per_device(object_tiles, probe, prop_phase, amplitudes, offsets, counts, step_size):
    n = probe.shape[1]
    rows, inner = object_tiles.shape[2:]
    cos, sin = dft_table(n)
    tall = rows + 2 * H
    smem = pl.BlockSpec(memory_space=pltpu.SMEM)
    anywhere = pl.BlockSpec(memory_space=pl.ANY)
    on_chip = pl.BlockSpec(memory_space=pltpu.VMEM)
    vmem = lambda *shape, kind=F32: pltpu.VMEM(shape, kind)
    block = vmem(2, 2, H, n)
    long = 2 * tall - n - 2 * H
    scratch = (
        [vmem(2, SUBLANES, LANES, kind=jnp.int32), vmem(4, 2, SUBLANES, LANES, kind=jnp.int32)]
        + [vmem(2, n, n), vmem(2, n, n)]
        + [vmem(n, n, kind=BF16)] * 3
        + [vmem(2 * n, 2 * n, kind=BF16)] * 2
        + [vmem(2 * n, n, kind=BF16), vmem(n, 2 * n, kind=BF16), vmem(2, n, n)]
        + [vmem(2, 2, rows, H)] * 2
        + [vmem(2, n // LANES, tall, LANES)] * 2
        + [block] * 4
        + [vmem(2, n // LANES, long, LANES)] * 2
        + [block] * 2
        + [vmem(2, 2, n, H)] * 2
        + [vmem(2, long, H)] * 4
        + [vmem(2, 2, H, 2 * H)] * 2
        + [pltpu.SemaphoreType.DMA((REMOTES,))] * 2
        + [pltpu.SemaphoreType.DMA((LOCALS,))]
    )
    done = pl.pallas_call(
        step_kernel,
        in_specs=[smem] * 3 + [anywhere] * 6,
        out_specs=on_chip,
        out_shape=pltpu.VMEM(object_tiles.shape, F32),
        scratch_shapes=scratch,
        name="step",
        compiler_params=pltpu.CompilerParams(
            collective_id=0, has_side_effects=True, vmem_limit_bytes=VMEM_LIMIT
        ),
    )(offsets[0, 0, 0], counts[0], step_size, object_tiles, probe, prop_phase, amplitudes, cos, sin)
    return pl.pallas_call(
        write_kernel,
        in_specs=[on_chip],
        out_specs=anywhere,
        out_shape=jax.ShapeDtypeStruct(object_tiles.shape, F32),
        scratch_shapes=[pltpu.SemaphoreType.DMA((4,))],
        name="write",
        compiler_params=pltpu.CompilerParams(vmem_limit_bytes=1 << 20),
    )(done)


VMEM_LIMIT = 54 << 20


def solution(mesh):
    return jax.shard_map(
        per_device,
        mesh=mesh,
        in_specs=(
            P(None, None, "rows", "cols"),
            P(),
            P(),
            P("rows", "cols", None, None, None),
            P("rows", "cols", None, None),
            P("rows", "cols"),
            P(),
        ),
        out_specs=P(None, None, "rows", "cols"),
        check_vma=False,
    )
```

time: 111 us -> 82.8 us (0.75)
  the two profiles are of different devices: /device:TPU:12 before, /device:TPU:3 now
where the time goes in v1:
time: 82.8 us; the launch traced here: 82.7 us
  Pallas kernels  81.9 us (99%)
    pallas_call x1, Pallas kernels, per_device(): pl.pallas_call(step_kernel, in_specs=[smem] * 3 + [anywhere] * 6, out_spe...  78.2 us
    pallas_call x1, Pallas kernels, per_device(): pl.pallas_call(write_kernel, in_specs=[on_chip], out_specs=anywhere, out_...  3.7 us

profile of v1, /device:TPU:3, one launch (start us, length us, event | category | flops | bytes accessed | tf_op | source)
XLA Modules:
  0.0 82.7 jit_solution(13275851379894362005)
XLA Ops:
  0.7 78.2 %step.1.done = f32[2,2,768,768]{3,2,1,0:T(8,128)S(1)} custom-call(s32[2]{0:T(128)} %bitcast.3, s32[1]{0:T(128)} %bitcast.2.count_ref, f32[2]{0:T(128)} %step_ref.1, f32[2,2,768,768]{3,2,1,0:T(8,128)} %obj.1, f32[2,512,512]{2,1,0:T(8,128)} %probe_in.1, f32[512,512]{1,0:T(8,128)} %phase_in.1, bf16[1,1,1,512,512]{4,3,2,1,0:T(8,128)(2,1)} %amp_in.1, ...), custom_call_target="tpu_custom_call" | custom-call | tf_op jit(solution)/shard_map/step/pallas_call | solution.py:605
  78.8 3.7 %write.1 = f32[2,2,768,768]{3,2,1,0:T(8,128)} custom-call(f32[2,2,768,768]{3,2,1,0:T(8,128)S(1)} %step.1.done), custom_call_target="tpu_custom_call" | custom-call | tf_op jit(solution)/shard_map/write/pallas_call | solution.py:616

commit v2 on v1

--- a/solution.py
+++ b/solution.py
@@ -11,7 +11,11 @@
 H = 128
 LANES = 128
 SUBLANES = 8
-PARTS = 2
+EVEN_CHUNKS = [(p, h, H // 2) for p in range(2) for h in (0, H // 2)]
+FIRST_SMALL = [(0, 0, H // 4), (0, H // 4, H // 4)] + EVEN_CHUNKS[1:]
+LAST_SMALL = EVEN_CHUNKS[:3] + [(1, H // 2, H // 4), (1, 3 * H // 4, H // 4)]
+FORWARD = (FIRST_SMALL, EVEN_CHUNKS)
+BACKWARD = (LAST_SMALL, EVEN_CHUNKS)
 F32 = jnp.float32
 BF16 = jnp.bfloat16
 MESH = pl.DeviceIdType.MESH
@@ -80,14 +84,14 @@
         pl.when(self.there)(lambda: self.copy.wait_send())
 
 
-REMOTES = 4 + 2 * (8 + 12 * PARTS)
+REMOTES = 22 + 2 * sum(map(len, FORWARD)) + 4 * sum(map(len, BACKWARD))
 LOCALS = 5 + 2 * 3
 
 
 def step_kernel(
     offs_ref, count_ref, step_ref, obj, probe_in, phase_in, amp_in, cos_in, sin_in, out,
     meta, near, probe, k, amp, cos, sin, fwd, bwd, src, mid, psi,
-    hl, hr, body0, body1, xs, xr, ss, sr, gz0, gz1,
+    hl, hr, body0, body1, xs, xr, ss, sr, placed, ends_raw, share,
     orr, ox, own_l, own_r, gl0, gl1, gr0, gr1, near_l, near_r,
     sends, receives, locals_,
 ):
@@ -97,7 +101,7 @@
     tall = tile_rows + 2 * H
     half = (tall - n) // 2
     last = tile_rows - H
-    bodies, gzs, gls, grs = (body0, body1), (gz0, gz1), (gl0, gl1), (gr0, gr1)
+    bodies, gls, grs = (body0, body1), (gl0, gl1), (gr0, gr1)
 
     me_r, me_c = lax.axis_index("rows"), lax.axis_index("cols")
     n_r, n_c = lax.axis_size("rows"), lax.axis_size("cols")
@@ -186,30 +190,33 @@
         to_right(meta, near.at[2]),
         to_left(meta, near.at[3]),
     ]
-    halos = [
-        [
-            [
-                to_right(obj.at[s, :, at, inner - H :], hl.at[s, :, at, :]),
-                to_left(obj.at[s, :, at, 0:H], hr.at[s, :, at, :]),
-            ]
-            for at in pieces
+    def halo(s, at, p=slice(None)):
+        return [
+            to_right(obj.at[s, p, at, inner - H :], hl.at[s, p, at, :]),
+            to_left(obj.at[s, p, at, 0:H], hr.at[s, p, at, :]),
         ]
-        for s in range(2)
-    ]
+
+    halos = [[halo(s, at) for at in pieces] if s else [None] + [halo(s, at) for at in pieces[1:]] for s in range(2)]
+    halo_first = [halo(0, far_rows, p) for p in range(2)]
+    halos[0][0] = halo_first[0] + halo_first[1]
     for group in (metas, halos[0][0], halos[0][1], halos[1][0], halos[1][1], halos[0][2], halos[1][2]):
         for c in group:
             c.start()
 
-    for lo, hi in ((0, first_row), (first_row + n, gz0.shape[2])):
-
-        @pl.loop(0, n // LANES)
-        def _(q, lo=lo, hi=hi):
-            for gz in gzs:
-                for p in range(2):
-                    gz[p, q, lo:hi, :] = jnp.zeros((hi - lo, LANES), F32)
-
+    tiles = n // LANES + 1
+    long = placed.shape[1]
+
+    @pl.loop(0, 2 * tiles)
+    def _(q):
+        placed[q, :first_row, :] = jnp.zeros((first_row, LANES), F32)
+        placed[q, first_row + n :, :] = jnp.zeros((first_row, LANES), F32)
+
+    placed[2 * tiles] = jnp.zeros((long, LANES), F32)
+    for lo, hi in ((0, first_row), (first_row + n, long)):
         for ref in gls + grs:
             ref[:, lo:hi, :] = jnp.zeros((2, hi - lo, H), F32)
+    for lo in (0, 3 * H):
+        ends_raw[:, :, lo : lo + H, :] = jnp.zeros((2, n // LANES, H, LANES), F32)
 
     my_row, my_col = offs_ref[0], offs_ref[1]
     weight = jnp.where(count_ref[0] > 0, 1.0, 0.0).astype(F32)
@@ -234,26 +241,24 @@
         for q in range(n // LANES):
             field[part, q, rows, :] = value[:, q * LANES : (q + 1) * LANES]
 
-    size = H // PARTS
-    chunks = [(p, h) for p in range(2) for h in range(PARTS)]
-    lines = lambda h: pl.ds(h * size, size)
-
-    outers = [
-        {(p, h): copies.remote(xs.at[s, p, lines(h)], xr.at[s, p, lines(h)], has_outward, has_inward, outward) for p, h in chunks}
-        for s in range(2)
+    along = lambda chunks, source, target, there, here, device: [
+        copies.remote(source.at[p, pl.ds(h, size)], target.at[p, pl.ds(h, size)], there, here, device)
+        for p, h, size in chunks
     ]
-    inners = [
-        {(p, h): copies.remote(ss.at[s, p, lines(h)], sr.at[s, p, lines(h)], always, always, partner) for p, h in chunks}
-        for s in range(2)
-    ]
+    outers = [along(FORWARD[s], xs.at[s], xr.at[s], has_outward, has_inward, outward) for s in range(2)]
+    inners = [along(FORWARD[s], ss.at[s], sr.at[s], always, always, partner) for s in range(2)]
     for s in range(2):
         loads[s][0].wait()
-        for c in halos[s][0]:
-            c.arrived()
-        for p, h in chunks:
-            at = pl.ds(pl.multiple_of(odd * last + h * size, size), size)
-            xs[s, p, lines(h)] = take_columns(s, p, at, far_col)
-            outers[s][p, h].start()
+        if s:
+            for c in halos[s][0]:
+                c.arrived()
+        for i, (p, h, size) in enumerate(FORWARD[s]):
+            if not s and h == 0:
+                for c in halo_first[p]:
+                    c.arrived()
+            at = pl.ds(pl.multiple_of(odd * last + h, SUBLANES), size)
+            xs[s, p, pl.ds(h, size)] = take_columns(s, p, at, far_col)
+            outers[s][i].start()
     for s in range(2):
         loads[s][1].wait()
         for c in halos[s][1]:
@@ -263,11 +268,13 @@
 
     mate_near = jnp.where(even, mate_row <= half, mate_row > half)
 
-    def pass_on(s, i):
-        p, h = chunks[i]
-        outers[s][p, h].arrived()
-        ss[s, p, lines(h)] = jnp.where(mate_near, ss[s, p, lines(h)], xr[s, p, lines(h)])
-        inners[s][p, h].start()
+    def pass_on(s, *which):
+        for i in which:
+            p, h, size = FORWARD[s][i]
+            at = pl.ds(h, size)
+            outers[s][i].arrived()
+            ss[s, p, at] = jnp.where(mate_near, ss[s, p, at], xr[s, p, at])
+            inners[s][i].start()
 
     for c in load_small[:3]:
         c.wait()
@@ -295,23 +302,23 @@
         for c in halos[s][2]:
             c.arrived()
 
-    count = len(chunks)
+    pass_on(0, 0)
     make_tables(cos, sin, fwd, bwd)
-    pass_on(0, 0)
+    pass_on(0, 1)
     propagator(0, n // 2)
-    pass_on(0, 1)
+    pass_on(0, 2)
     propagator(n // 2, n)
+    pass_on(0, 3)
     body_ready(0)
-    for i in range(2, count):
-        pass_on(0, i)
-        if i < 4:
-            fill_body(0, i - 2)
+    fill_body(0, 0)
+    pass_on(0, 4)
+    fill_body(0, 1)
     for c in load_small[3:]:
         c.wait()
 
     def halo_rows(s):
-        for p, h in chunks:
-            inners[s][p, h].arrived()
+        for c in inners[s]:
+            c.arrived()
         for p in range(2):
             block = sr[s, p]
             put_rows(bodies[s], p, slice(0, H), block)
@@ -327,6 +334,17 @@
             ).astype(BF16)
             for f in between[i : i + 1]:
                 f()
+
+    interior = ((H, n - H), (n + H, 2 * n - H))
+    exterior = ((0, H), (n - H, n + H), (2 * n - H, 2 * n))
+
+    def product(left, i, spans):
+        rows = slice(i * n, (i + 1) * n)
+        return jnp.dot(
+            jnp.concatenate([left[rows, a:b] for a, b in spans], axis=1),
+            jnp.concatenate([src[a:b, :] for a, b in spans], axis=0),
+            preferred_element_type=F32,
+        )
 
     def stage_two(right, spans, epilogue):
         rows = [mid[lo : lo + height, :] for lo, height in spans]
@@ -365,29 +383,31 @@
         psi[0, at, :] = re
         psi[1, at, :] = im
 
-    stage_one(fwd, (lambda: pass_on(1, 1),))
+    def exit_wave(lo, height):
+        at, low = full(lo, height)
+        b_re = window(1, 0, lo, height)
+        b_im = window(1, 1, lo, height)
+        p_re, p_im = psi[0, at, :], psi[1, at, :]
+        src[at, :] = (p_re * b_re - p_im * b_im).astype(BF16)
+        src[low, :] = (p_re * b_im + p_im * b_re).astype(BF16)
+
+    stage_one(fwd)
     stage_two(bwd, whole, propagate)
-    for i in range(2, count // 2 + 1):
-        pass_on(1, i)
+    pass_on(1, 1)
     stage_one(bwd)
     body_ready(1)
     fill_body(1, 0)
-    for i in range(count // 2 + 1, count):
-        pass_on(1, i)
+    pass_on(1, 2)
     stage_two(fwd, whole, keep)
+    pass_on(1, 3)
     fill_body(1, 1)
-
+    for lo in range(H, n - H, H):
+        exit_wave(lo, H)
+    for i in range(2):
+        share[i] = product(fwd, i, interior)
     halo_rows(1)
-
-    @pl.loop(0, n // H)
-    def _(i):
-        at = pl.ds(pl.multiple_of(i * H, H), H)
-        low = pl.ds(pl.multiple_of(n + i * H, H), H)
-        b_re = window(1, 0, i * H, H)
-        b_im = window(1, 1, i * H, H)
-        p_re, p_im = psi[0, at, :], psi[1, at, :]
-        src[at, :] = (p_re * b_re - p_im * b_im).astype(BF16)
-        src[low, :] = (p_re * b_im + p_im * b_re).astype(BF16)
+    for lo in (0, n - H):
+        exit_wave(lo, H)
 
     def detect(lo, height, re, im):
         at, low = full(lo, height)
@@ -395,15 +415,23 @@
         src[at, :] = (re * factor).astype(BF16)
         src[low, :] = (im * factor).astype(BF16)
 
+    turn = lax.rem(my_col, LANES)
+
     def emit(s, p, lo, height, value):
-        put_rows(gzs[s], p, pl.ds(first_row + lo, height), value)
         lane = lax.broadcasted_iota(jnp.int32, (height, LANES), 1)
-        turn = lax.rem(my_col, LANES)
-        at = pl.ds(lo, height)
-        own_l[s, p, at, :] = jnp.where(lane >= my_col, pltpu.roll(value[:, :LANES], turn, axis=1), 0.0)
-        own_r[s, p, at, :] = jnp.where(
-            lane < my_col - (inner + H - n), pltpu.roll(value[:, n - LANES :], turn, axis=1), 0.0
-        )
+        zero = jnp.zeros((height, LANES), F32)
+        pieces = [value[:, q * LANES : (q + 1) * LANES] for q in range(n // LANES)]
+        turned = [pltpu.roll(piece, turn, axis=1) for piece in pieces]
+        at = pl.ds(first_row + lo, height)
+        for q in range(tiles):
+            before = turned[q - 1] if q else zero
+            here = turned[q] if q < tiles - 1 else zero
+            placed[p * tiles + q, at, :] = jnp.where(lane >= turn, here, before)
+        own_l[s, p, pl.ds(lo, height), :] = jnp.where(lane >= my_col, turned[0], 0.0)
+        own_r[s, p, pl.ds(lo, height), :] = jnp.where(lane < my_col - (inner + H - n), turned[-1], 0.0)
+        if (lo, height) in ends:
+            for q, piece in enumerate(pieces):
+                ends_raw[p, q, pl.ds(H if lo == 0 else 2 * H, H), :] = piece
 
     def spread(lo, height, re, im):
         at, low = full(lo, height)
@@ -415,14 +443,8 @@
         src[at, :] = (b_re * re + b_im * im).astype(BF16)
         src[low, :] = (b_re * im - b_im * re).astype(BF16)
 
-    spills = [
-        {(p, h): copies.remote(ss.at[s, p, lines(h)], orr.at[s, p, lines(h)], always, always, partner) for p, h in chunks}
-        for s in range(2)
-    ]
-    relays = [
-        {(p, h): copies.remote(orr.at[s, p, lines(h)], ox.at[s, p, lines(h)], has_inward, has_outward, inward) for p, h in chunks}
-        for s in range(2)
-    ]
+    spills = [along(BACKWARD[s], ss.at[s], orr.at[s], always, always, partner) for s in range(2)]
+    relays = [along(BACKWARD[s], orr.at[s], ox.at[s], has_inward, has_outward, inward) for s in range(2)]
     early = [
         [
             to_left(own_l.at[s], grs[s].at[:, first_row : first_row + n, :]),
@@ -431,26 +453,29 @@
         for s in range(2)
     ]
     lates = [
-        {
-            (p, h): [
-                to_left(xs.at[s, p, lines(h), : 2 * H], near_r.at[s, p, lines(h)]),
-                to_right(xs.at[s, p, lines(h), 2 * H : 4 * H], near_l.at[s, p, lines(h)]),
+        [
+            [
+                to_left(xs.at[s, p, pl.ds(h, size), : 2 * H], near_r.at[s, p, pl.ds(h, size)]),
+                to_right(xs.at[s, p, pl.ds(h, size), 2 * H : 4 * H], near_l.at[s, p, pl.ds(h, size)]),
             ]
-            for p, h in chunks
-        }
+            for p, h, size in BACKWARD[s]
+        ]
         for s in range(2)
     ]
 
     def spill(s):
-        start = jnp.where(my_row <= half, first_row - my_row, first_row + tile_rows + H - my_row)
-        for p, h in chunks:
-            inners[s][p, h].sent()
-            ss[s, p, lines(h)] = take_rows(gzs[s], p, start + h * size, size)
-            spills[s][p, h].start()
-
-    def relay(s, i):
-        spills[s][chunks[i]].arrived()
-        relays[s][chunks[i]].start()
+        lower = tile_rows + 4 * H - n - jnp.maximum(my_row, tall - n - H)
+        start = jnp.where(my_row <= half, H - jnp.minimum(my_row, H), lower)
+        for c in inners[s]:
+            c.sent()
+        for i, (p, h, size) in enumerate(BACKWARD[s]):
+            ss[s, p, pl.ds(h, size)] = take_rows(ends_raw, p, start + h, size)
+            spills[s][i].start()
+
+    def relay(s, *which):
+        for i in which:
+            spills[s][i].arrived()
+            relays[s][i].start()
 
     def back(lo, height, re, im):
         at, low = full(lo, height)
@@ -464,7 +489,66 @@
         emit(0, 0, lo, height, weight * (q_re * re + q_im * im))
         emit(0, 1, lo, height, weight * (q_re * im - q_im * re))
 
-    stage_one(fwd)
+    spread_out = lambda block, start: pltpu.roll(
+        jnp.concatenate([block, jnp.zeros((block.shape[0], wide - n), F32)], axis=1), start, axis=1
+    )
+
+    column = sum(jnp.where(my_col >= q * LANES, 1, 0) for q in range(1, (wide - n) // LANES + 1))
+
+    def place_own(s, p):
+        @pl.loop(0, tile_rows // H)
+        def _(i):
+            at = pl.ds(pl.multiple_of(i * H, H), H)
+            for j in range(inner // LANES):
+                tile = j + H // LANES - column
+                inside = jnp.logical_and(tile >= 0, tile < tiles)
+                tile = jnp.where(inside, p * tiles + tile, 2 * tiles)
+                block = placed[tile, pl.ds(tall - n - my_row + i * H, H), :]
+                lanes = slice(j * LANES, (j + 1) * LANES)
+                out[s, p, at, lanes] -= step_ref[s] * block
+
+    def place_near(s, i):
+        p, h, size = BACKWARD[s][i]
+        at = pl.ds(h, size)
+        relays[s][i].arrived()
+        for e, mine, start in (
+            (0, jnp.logical_and(has_above, above_row > half), above_col),
+            (1, jnp.logical_and(has_below, below_row <= half), below_col),
+        ):
+            outer = even if e == 0 else jnp.logical_not(even)
+            block = jnp.where(outer, ox[s, p, at], orr[s, p, at])
+            block = spread_out(jnp.where(mine, block, jnp.zeros_like(block)), start)
+            xs[s, p, at, e * H : (e + 1) * H] = block[:, :H]
+            xs[s, p, at, (2 + e) * H : (3 + e) * H] = block[:, H + inner :]
+            rows = pl.ds(e * last + h, size)
+            out[s, p, rows, :] -= step_ref[s] * block[:, H : H + inner]
+        for c in lates[s][i]:
+            c.start()
+
+    def sides(s):
+        for c in early[s]:
+            c.arrived()
+        for p in range(2):
+
+            @pl.loop(0, tile_rows // H)
+            def _(i, p=p):
+                at = pl.ds(pl.multiple_of(i * H, H), H)
+                from_left = gls[s][p, pl.ds(tall - n - left_row + i * H, H), :]
+                from_right = grs[s][p, pl.ds(tall - n - right_row + i * H, H), :]
+                out[s, p, at, :H] -= step_ref[s] * from_left
+                out[s, p, at, inner - H :] -= step_ref[s] * from_right
+
+    def corners(s, i):
+        p, h, size = BACKWARD[s][i]
+        for c in lates[s][i]:
+            c.arrived()
+        for e in range(2):
+            at = pl.ds(e * last + h, size)
+            out[s, p, at, :H] -= step_ref[s] * near_l[s, p, pl.ds(h, size), e * H : (e + 1) * H]
+            out[s, p, at, inner - H :] -= step_ref[s] * near_r[s, p, pl.ds(h, size), e * H : (e + 1) * H]
+
+    for i in range(2):
+        mid[:, i * n : (i + 1) * n] = (share[i] + product(fwd, i, exterior)).astype(BF16)
     stage_two(bwd, whole, detect)
     stage_one(bwd)
     stage_two(fwd, ends, spread)
@@ -475,86 +559,39 @@
     stage_one(fwd)
     relay(1, 0)
     stage_two(bwd, whole, back)
-    for i in range(1, count // 2):
-        relay(1, i)
+    place_own(1, 0)
+    relay(1, 1)
+    place_own(1, 1)
     stage_one(bwd)
     stage_two(fwd, ends, finish)
     spill(0)
+    relay(1, 2)
     stage_two(fwd, middle, finish)
     for c in early[0]:
         c.start()
-
-    spread_out = lambda block, start: pltpu.roll(
-        jnp.concatenate([block, jnp.zeros((block.shape[0], wide - n), F32)], axis=1), start, axis=1
-    )
-
-    def place_own(s, p):
-        @pl.loop(0, tile_rows // H)
-        def _(i):
-            block = spread_out(take_rows(gzs[s], p, tall - n - my_row + i * H, H), my_col)
-            at = pl.ds(pl.multiple_of(i * H, H), H)
-            out[s, p, at, :] -= step_ref[s] * block[:, H : H + inner]
-
-    def place_near(s, i):
-        p, h = chunks[i]
-        relays[s][p, h].arrived()
-        outers[s][p, h].sent()
-        for e, mine, start in (
-            (0, jnp.logical_and(has_above, above_row > half), above_col),
-            (1, jnp.logical_and(has_below, below_row <= half), below_col),
-        ):
-            outer = even if e == 0 else jnp.logical_not(even)
-            block = jnp.where(outer, ox[s, p, lines(h)], orr[s, p, lines(h)])
-            block = spread_out(jnp.where(mine, block, jnp.zeros_like(block)), start)
-            xs[s, p, lines(h), e * H : (e + 1) * H] = block[:, :H]
-            xs[s, p, lines(h), (2 + e) * H : (3 + e) * H] = block[:, H + inner :]
-            at = pl.ds(e * last + h * size, size)
-            out[s, p, at, :] -= step_ref[s] * block[:, H : H + inner]
-        for c in lates[s][p, h]:
-            c.start()
-
-    def sides(s):
-        for c in early[s]:
-            c.arrived()
-        for p in range(2):
-
-            @pl.loop(0, tile_rows // H)
-            def _(i, p=p):
-                at = pl.ds(pl.multiple_of(i * H, H), H)
-                from_left = gls[s][p, pl.ds(tall - n - left_row + i * H, H), :]
-                from_right = grs[s][p, pl.ds(tall - n - right_row + i * H, H), :]
-                out[s, p, at, :H] -= step_ref[s] * from_left
-                out[s, p, at, inner - H :] -= step_ref[s] * from_right
-
-    def corners(s, i):
-        p, h = chunks[i]
-        for c in lates[s][p, h]:
-            c.arrived()
-        for e in range(2):
-            at = pl.ds(e * last + h * size, size)
-            out[s, p, at, :H] -= step_ref[s] * near_l[s, p, lines(h), e * H : (e + 1) * H]
-            out[s, p, at, inner - H :] -= step_ref[s] * near_r[s, p, lines(h), e * H : (e + 1) * H]
-
-    for i in range(count // 2, count):
-        relay(1, i)
-    place_own(1, 0)
-    place_own(1, 1)
-    for i in range(count):
-        place_near(1, i)
+    for c in outers[0] + outers[1]:
+        c.sent()
+    relay(1, 3)
+    place_near(1, 0)
+    place_near(1, 1)
+    place_own(0, 0)
     relay(0, 0)
-    place_own(0, 0)
+    place_near(1, 2)
+    place_near(1, 3)
+    place_own(0, 1)
     relay(0, 1)
-    place_own(0, 1)
     sides(1)
-    for i in range(2, count):
-        relay(0, i)
-        place_near(0, i - 2)
-    for i in range(count):
+    relay(0, 2)
+    for i in range(4):
         corners(1, i)
+    place_near(0, 0)
+    relay(0, 3)
+    place_near(0, 1)
+    relay(0, 4)
     sides(0)
-    for i in range(count - 2, count):
+    for i in range(2, 5):
         place_near(0, i)
-    for i in range(count):
+    for i in range(5):
         corners(0, i)
 
     for c in copies.remotes:
@@ -565,9 +602,10 @@
 
 def write_kernel(done, out, sems):
     copies = []
-    for s in range(2):
-        for p in range(2):
-            copies.append(pltpu.make_async_copy(done.at[s, p], out.at[s, p], sems.at[2 * s + p]))
+    rows = done.shape[2] // 3
+    for i in range(12):
+        at = (i // 6, i // 3 % 2, pl.ds(i % 3 * rows, rows))
+        copies.append(pltpu.make_async_copy(done.at[at], out.at[at], sems.at[i]))
     for c in copies:
         c.start()
     for c in copies:
@@ -594,7 +632,7 @@
         + [vmem(2, 2, rows, H)] * 2
         + [vmem(2, n // LANES, tall, LANES)] * 2
         + [block] * 4
-        + [vmem(2, n // LANES, long, LANES)] * 2
+        + [vmem(2 * (n // LANES + 1) + 1, long, LANES), vmem(2, n // LANES, 4 * H, LANES), vmem(2, n, n)]
         + [block] * 2
         + [vmem(2, 2, n, H)] * 2
         + [vmem(2, long, H)] * 4
@@ -618,7 +656,7 @@
         in_specs=[on_chip],
         out_specs=anywhere,
         out_shape=jax.ShapeDtypeStruct(object_tiles.shape, F32),
-        scratch_shapes=[pltpu.SemaphoreType.DMA((4,))],
+        scratch_shapes=[pltpu.SemaphoreType.DMA((12,))],
         name="write",
         compiler_params=pltpu.CompilerParams(vmem_limit_bytes=1 << 20),
     )(done)

time: 82.8 us -> 80.9 us (0.977)
  Pallas kernels: 81.9 us -> 79.9 us
    pallas_call x1, Pallas kernels: 78.2 us -> 76.2 us  [per_device(): pl.pallas_call(step_kernel, in_specs=[smem] * 3 + [anywhere] * 6, out_spe...]
where the time goes in v2:
time: 80.9 us; the launch traced here: 80.7 us
  Pallas kernels  79.9 us (99%)
  between operations  0.82 us (1%)
    pallas_call x1, Pallas kernels, per_device(): pl.pallas_call(step_kernel, in_specs=[smem] * 3 + [anywhere] * 6, out_spe...  76.2 us
    pallas_call x1, Pallas kernels, per_device(): pl.pallas_call(write_kernel, in_specs=[on_chip], out_specs=anywhere, out_...  3.72 us

profile of v2, /device:TPU:3, one launch (start us, length us, event | category | flops | bytes accessed | tf_op | source)
XLA Modules:
  0.0 80.7 jit_solution(12443445121618865542)
XLA Ops:
  0.7 76.2 %step.1.done = f32[2,2,768,768]{3,2,1,0:T(8,128)S(1)} custom-call(s32[2]{0:T(128)} %bitcast.3, s32[1]{0:T(128)} %bitcast.2.count_ref, f32[2]{0:T(128)} %step_ref.1, f32[2,2,768,768]{3,2,1,0:T(8,128)} %obj.1, f32[2,512,512]{2,1,0:T(8,128)} %probe_in.1, f32[512,512]{1,0:T(8,128)} %phase_in.1, bf16[1,1,1,512,512]{4,3,2,1,0:T(8,128)(2,1)} %amp_in.1, ...), custom_call_target="tpu_custom_call" | custom-call | tf_op jit(solution)/shard_map/step/pallas_call | solution.py:643
  76.8 3.7 %write.1 = f32[2,2,768,768]{3,2,1,0:T(8,128)} custom-call(f32[2,2,768,768]{3,2,1,0:T(8,128)S(1)} %step.1.done), custom_call_target="tpu_custom_call" | custom-call | tf_op jit(solution)/shard_map/write/pallas_call | solution.py:654

commit v3 on v2

--- a/solution.py
+++ b/solution.py
@@ -12,9 +12,8 @@
 LANES = 128
 SUBLANES = 8
 EVEN_CHUNKS = [(p, h, H // 2) for p in range(2) for h in (0, H // 2)]
-FIRST_SMALL = [(0, 0, H // 4), (0, H // 4, H // 4)] + EVEN_CHUNKS[1:]
-LAST_SMALL = EVEN_CHUNKS[:3] + [(1, H // 2, H // 4), (1, 3 * H // 4, H // 4)]
-FORWARD = (FIRST_SMALL, EVEN_CHUNKS)
+LAST_SMALL = EVEN_CHUNKS[:3] + [(1, H // 2, H // 4), (1, 3 * H // 4, H // 8), (1, 7 * H // 8, H // 8)]
+FORWARD = (EVEN_CHUNKS[:3] + [(1, H // 2, H // 4), (1, 3 * H // 4, H // 4)], LAST_SMALL)
 BACKWARD = (LAST_SMALL, EVEN_CHUNKS)
 F32 = jnp.float32
 BF16 = jnp.bfloat16
@@ -302,19 +301,19 @@
         for c in halos[s][2]:
             c.arrived()
 
+    make_tables(cos, sin, fwd, bwd)
+    propagator(0, n // 2)
     pass_on(0, 0)
-    make_tables(cos, sin, fwd, bwd)
+    propagator(n // 2, n)
     pass_on(0, 1)
-    propagator(0, n // 2)
+    for c in load_small[3:]:
+        c.wait()
     pass_on(0, 2)
-    propagator(n // 2, n)
-    pass_on(0, 3)
     body_ready(0)
     fill_body(0, 0)
+    pass_on(0, 3)
+    fill_body(0, 1)
     pass_on(0, 4)
-    fill_body(0, 1)
-    for c in load_small[3:]:
-        c.wait()
 
     def halo_rows(s):
         for c in inners[s]:
@@ -359,18 +358,34 @@
     ends = [(0, H), (n - H, H)]
     middle = [(H, n - 2 * H)]
 
-    halo_rows(0)
-    pass_on(1, 0)
-
-    @pl.loop(0, n // H)
-    def _(i):
-        at = pl.ds(pl.multiple_of(i * H, H), H)
-        low = pl.ds(pl.multiple_of(n + i * H, H), H)
-        a_re = window(0, 0, i * H, H)
-        a_im = window(0, 1, i * H, H)
+    def entry_wave(lo, height):
+        at, low = full(lo, height)
+        a_re = window(0, 0, lo, height)
+        a_im = window(0, 1, lo, height)
         q_re, q_im = probe[0, at, :], probe[1, at, :]
         src[at, :] = (q_re * a_re - q_im * a_im).astype(BF16)
         src[low, :] = (q_re * a_im + q_im * a_re).astype(BF16)
+
+    def first_product(wave, arrive):
+        for lo in range(H, n - H, H):
+            wave(lo, H)
+        for i in range(2):
+            share[i] = product(fwd, i, interior)
+        arrive()
+        for lo in (0, n - H):
+            wave(lo, H)
+        for i in range(2):
+            mid[:, i * n : (i + 1) * n] = (share[i] + product(fwd, i, exterior)).astype(BF16)
+
+    def first_halo():
+        pass_on(1, 0)
+        halo_rows(0)
+
+    def second_halo():
+        pass_on(1, 5)
+        halo_rows(1)
+
+    first_product(entry_wave, first_halo)
 
     def propagate(lo, height, re, im):
         at, low = full(lo, height)
@@ -391,23 +406,16 @@
         src[at, :] = (p_re * b_re - p_im * b_im).astype(BF16)
         src[low, :] = (p_re * b_im + p_im * b_re).astype(BF16)
 
-    stage_one(fwd)
     stage_two(bwd, whole, propagate)
     pass_on(1, 1)
     stage_one(bwd)
     body_ready(1)
     fill_body(1, 0)
+    fill_body(1, 1)
     pass_on(1, 2)
     stage_two(fwd, whole, keep)
-    pass_on(1, 3)
-    fill_body(1, 1)
-    for lo in range(H, n - H, H):
-        exit_wave(lo, H)
-    for i in range(2):
-        share[i] = product(fwd, i, interior)
-    halo_rows(1)
-    for lo in (0, n - H):
-        exit_wave(lo, H)
+    pass_on(1, 3, 4)
+    first_product(exit_wave, second_halo)
 
     def detect(lo, height, re, im):
         at, low = full(lo, height)
@@ -547,8 +555,6 @@
             out[s, p, at, :H] -= step_ref[s] * near_l[s, p, pl.ds(h, size), e * H : (e + 1) * H]
             out[s, p, at, inner - H :] -= step_ref[s] * near_r[s, p, pl.ds(h, size), e * H : (e + 1) * H]
 
-    for i in range(2):
-        mid[:, i * n : (i + 1) * n] = (share[i] + product(fwd, i, exterior)).astype(BF16)
     stage_two(bwd, whole, detect)
     stage_one(bwd)
     stage_two(fwd, ends, spread)
@@ -557,41 +563,39 @@
     for c in early[1]:
         c.start()
     stage_one(fwd)
-    relay(1, 0)
     stage_two(bwd, whole, back)
     place_own(1, 0)
-    relay(1, 1)
     place_own(1, 1)
+    relay(1, 0)
     stage_one(bwd)
     stage_two(fwd, ends, finish)
     spill(0)
-    relay(1, 2)
+    relay(1, 1)
     stage_two(fwd, middle, finish)
     for c in early[0]:
         c.start()
     for c in outers[0] + outers[1]:
         c.sent()
+    place_own(0, 0)
+    place_own(0, 1)
+    relay(1, 2)
+    place_near(1, 0)
     relay(1, 3)
-    place_near(1, 0)
     place_near(1, 1)
-    place_own(0, 0)
+    sides(1)
     relay(0, 0)
     place_near(1, 2)
     place_near(1, 3)
-    place_own(0, 1)
     relay(0, 1)
-    sides(1)
+    sides(0)
     relay(0, 2)
     for i in range(4):
         corners(1, i)
     place_near(0, 0)
-    relay(0, 3)
-    place_near(0, 1)
-    relay(0, 4)
-    sides(0)
-    for i in range(2, 5):
+    relay(0, 3, 4, 5)
+    for i in range(1, 6):
         place_near(0, i)
-    for i in range(5):
+    for i in range(6):
         corners(0, i)
 
     for c in copies.remotes:

time: 80.9 us -> 83.9 us (1.037)
  Pallas kernels: 79.9 us -> 82.9 us
    pallas_call x1, Pallas kernels: 76.2 us -> 79.2 us  [per_device(): pl.pallas_call(step_kernel, in_specs=[smem] * 3 + [anywhere] * 6, out_spe...]
where the time goes in v3:
time: 83.9 us; the launch traced here: 83.8 us
  Pallas kernels  82.9 us (99%)
    pallas_call x1, Pallas kernels, per_device(): pl.pallas_call(step_kernel, in_specs=[smem] * 3 + [anywhere] * 6, out_spe...  79.2 us
    pallas_call x1, Pallas kernels, per_device(): pl.pallas_call(write_kernel, in_specs=[on_chip], out_specs=anywhere, out_...  3.72 us

profile of v3, /device:TPU:3, one launch (start us, length us, event | category | flops | bytes accessed | tf_op | source)
XLA Modules:
  0.0 83.8 jit_solution(6207873646689587387)
XLA Ops:
  0.7 79.2 %step.1.done = f32[2,2,768,768]{3,2,1,0:T(8,128)S(1)} custom-call(s32[2]{0:T(128)} %bitcast.3, s32[1]{0:T(128)} %bitcast.2.count_ref, f32[2]{0:T(128)} %step_ref.1, f32[2,2,768,768]{3,2,1,0:T(8,128)} %obj.1, f32[2,512,512]{2,1,0:T(8,128)} %probe_in.1, f32[512,512]{1,0:T(8,128)} %phase_in.1, bf16[1,1,1,512,512]{4,3,2,1,0:T(8,128)(2,1)} %amp_in.1, ...), custom_call_target="tpu_custom_call" | custom-call | tf_op jit(solution)/shard_map/step/pallas_call | solution.py:647
  79.9 3.7 %write.1 = f32[2,2,768,768]{3,2,1,0:T(8,128)} custom-call(f32[2,2,768,768]{3,2,1,0:T(8,128)S(1)} %step.1.done), custom_call_target="tpu_custom_call" | custom-call | tf_op jit(solution)/shard_map/write/pallas_call | solution.py:658

commit v4 on v2

--- a/solution.py
+++ b/solution.py
@@ -247,7 +247,7 @@
     ]
     outers = [along(FORWARD[s], xs.at[s], xr.at[s], has_outward, has_inward, outward) for s in range(2)]
     inners = [along(FORWARD[s], ss.at[s], sr.at[s], always, always, partner) for s in range(2)]
-    for s in range(2):
+    def send_far(s):
         loads[s][0].wait()
         if s:
             for c in halos[s][0]:
@@ -259,13 +259,16 @@
             at = pl.ds(pl.multiple_of(odd * last + h, SUBLANES), size)
             xs[s, p, pl.ds(h, size)] = take_columns(s, p, at, far_col)
             outers[s][i].start()
-    for s in range(2):
+
+    def take_mate(s):
         loads[s][1].wait()
         for c in halos[s][1]:
             c.arrived()
         for p in range(2):
             ss[s, p] = take_columns(s, p, mate_rows, mate_col)
 
+    send_far(0)
+    take_mate(0)
     mate_near = jnp.where(even, mate_row <= half, mate_row > half)
 
     def pass_on(s, *which):
@@ -276,9 +279,6 @@
             ss[s, p, at] = jnp.where(mate_near, ss[s, p, at], xr[s, p, at])
             inners[s][i].start()
 
-    for c in load_small[:3]:
-        c.wait()
-
     def propagator(lo, hi):
         @pl.loop(lo // LANES, hi // LANES)
         def _(i):
@@ -303,18 +303,20 @@
             c.arrived()
 
     pass_on(0, 0)
+    send_far(1)
+    pass_on(0, 1)
+    take_mate(1)
+    pass_on(0, 2)
+    for c in load_small:
+        c.wait()
     make_tables(cos, sin, fwd, bwd)
-    pass_on(0, 1)
     propagator(0, n // 2)
-    pass_on(0, 2)
+    pass_on(0, 3)
     propagator(n // 2, n)
-    pass_on(0, 3)
+    pass_on(0, 4)
     body_ready(0)
     fill_body(0, 0)
-    pass_on(0, 4)
     fill_body(0, 1)
-    for c in load_small[3:]:
-        c.wait()
 
     def halo_rows(s):
         for c in inners[s]:

time: 80.9 us -> 80.1 us (level)
  no operation moved by 1% of the time
where the time goes in v4:
time: 80.1 us; the launch traced here: 80 us
  Pallas kernels  79.2 us (99%)
  between operations  0.82 us (1%)
    pallas_call x1, Pallas kernels, per_device(): pl.pallas_call(step_kernel, in_specs=[smem] * 3 + [anywhere] * 6, out_spe...  75.5 us
    pallas_call x1, Pallas kernels, per_device(): pl.pallas_call(write_kernel, in_specs=[on_chip], out_specs=anywhere, out_...  3.72 us

profile of v4, /device:TPU:3, one launch (start us, length us, event | category | flops | bytes accessed | tf_op | source)
XLA Modules:
  0.0 80.0 jit_solution(1076208222158813902)
XLA Ops:
  0.7 75.5 %step.1.done = f32[2,2,768,768]{3,2,1,0:T(8,128)S(1)} custom-call(s32[2]{0:T(128)} %bitcast.3, s32[1]{0:T(128)} %bitcast.2.count_ref, f32[2]{0:T(128)} %step_ref.1, f32[2,2,768,768]{3,2,1,0:T(8,128)} %obj.1, f32[2,512,512]{2,1,0:T(8,128)} %probe_in.1, f32[512,512]{1,0:T(8,128)} %phase_in.1, bf16[1,1,1,512,512]{4,3,2,1,0:T(8,128)(2,1)} %amp_in.1, ...), custom_call_target="tpu_custom_call" | custom-call | tf_op jit(solution)/shard_map/step/pallas_call | solution.py:645
  76.1 3.7 %write.1 = f32[2,2,768,768]{3,2,1,0:T(8,128)} custom-call(f32[2,2,768,768]{3,2,1,0:T(8,128)S(1)} %step.1.done), custom_call_target="tpu_custom_call" | custom-call | tf_op jit(solution)/shard_map/write/pallas_call | solution.py:656

commit v5 on v4

--- a/solution.py
+++ b/solution.py
@@ -584,14 +584,15 @@
     relay(0, 1)
     sides(1)
     relay(0, 2)
-    for i in range(4):
-        corners(1, i)
     place_near(0, 0)
     relay(0, 3)
     place_near(0, 1)
     relay(0, 4)
+    place_near(0, 2)
+    for i in range(4):
+        corners(1, i)
     sides(0)
-    for i in range(2, 5):
+    for i in range(3, 5):
         place_near(0, i)
     for i in range(5):
         corners(0, i)

time: 80.1 us -> 79.6 us (level)
  no operation moved by 1% of the time
where the time goes in v5:
time: 79.6 us; the launch traced here: 79.4 us
  Pallas kernels  78.6 us (99%)
  between operations  0.82 us (1%)
    pallas_call x1, Pallas kernels, per_device(): pl.pallas_call(step_kernel, in_specs=[smem] * 3 + [anywhere] * 6, out_spe...  74.9 us
    pallas_call x1, Pallas kernels, per_device(): pl.pallas_call(write_kernel, in_specs=[on_chip], out_specs=anywhere, out_...  3.72 us

profile of v5, /device:TPU:3, one launch (start us, length us, event | category | flops | bytes accessed | tf_op | source)
XLA Modules:
  0.0 79.4 jit_solution(3370624640059267960)
XLA Ops:
  0.7 74.9 %step.1.done = f32[2,2,768,768]{3,2,1,0:T(8,128)S(1)} custom-call(s32[2]{0:T(128)} %bitcast.3, s32[1]{0:T(128)} %bitcast.2.count_ref, f32[2]{0:T(128)} %step_ref.1, f32[2,2,768,768]{3,2,1,0:T(8,128)} %obj.1, f32[2,512,512]{2,1,0:T(8,128)} %probe_in.1, f32[512,512]{1,0:T(8,128)} %phase_in.1, bf16[1,1,1,512,512]{4,3,2,1,0:T(8,128)(2,1)} %amp_in.1, ...), custom_call_target="tpu_custom_call" | custom-call | tf_op jit(solution)/shard_map/step/pallas_call | solution.py:646
  75.5 3.7 %write.1 = f32[2,2,768,768]{3,2,1,0:T(8,128)} custom-call(f32[2,2,768,768]{3,2,1,0:T(8,128)S(1)} %step.1.done), custom_call_target="tpu_custom_call" | custom-call | tf_op jit(solution)/shard_map/write/pallas_call | solution.py:657
